TPU v7x, 32 devices: a whole 2x2x4 slice. The times are simulated.
32 devices in a mesh: parts: 2 (over y), clus: 4 (over z), mem: 2 (over x), sub: 2 (over core).
Axes of the slice: x: 2, y: 2, z: 4, core: 2. Of those that a mesh axis runs over, the one named last changes fastest.
Arguments:
- embeddings: bfloat16 [4096, 1024], P(('parts', 'clus', 'mem', 'sub')), parts along dimension 0, as said below
- labels: int32 [4096], P(('parts', 'clus', 'mem', 'sub')), parts along dimension 0, may hold values from 0 to 15, as said below
- member_rank: int32 [4096], P(('parts', 'clus', 'mem', 'sub')), parts along dimension 0, may hold values from 0 to 2047, each once
Outputs:
- nearest: float32 [4096], P(('parts', 'clus', 'mem', 'sub')), parts along dimension 0
There are 2 independent parts, one for each index of `parts`. A program takes and returns all parts, laid end to end along the dimension named above; each array names one. Nothing has to cross between parts.
Inputs may be any that keep to these rules, and one draw needn't show every extreme that they name: `embeddings`: each row has unit length up to rounding. Among the rows of one device, at most 32 have labels in any one group of 2 consecutive clusters (label // 2); on every device some group has exactly 32.
All inputs are finite; a program needn't handle non-finite values.
Results may differ from a plain program's by a relative error of at most 0.0003.
Values may be sent and summed in bfloat16 or wider, within the bound.
A program may use at most 64 MiB of HBM per device.

v0:
```python
import math

import jax
import jax.numpy as jnp
from jax import lax
from jax.sharding import PartitionSpec as P

CLUS_GROUP = 2


def swapped(value, axis, stride):
    mask = 2**stride
    pairs = [(source, source ^ mask) for source in range(lax.axis_size(axis))]
    return lax.ppermute(value, axis, pairs)


def masked_best(row_emb, row_label, row_rank, col_emb, col_label, col_rank, want_columns):
    col_count = col_emb.shape[0]
    block_size = math.gcd(512, col_count)
    block_count = col_count // block_size
    emb_blocks = col_emb.reshape(block_count, block_size, col_emb.shape[1])
    label_blocks = col_label.reshape(block_count, block_size)
    rank_blocks = col_rank.reshape(block_count, block_size)

    def visit_block(running, column_piece):
        piece_emb, piece_label, piece_rank = column_piece
        scores = lax.dot_general(
            row_emb, piece_emb, (((1,), (1,)), ((), ())), preferred_element_type=jnp.float32
        )
        same_cluster = (row_label[:, None] == piece_label[None, :]) & (row_label[:, None] >= 0)
        earlier = piece_rank[None, :] < row_rank[:, None]
        row_best = jnp.max(jnp.where(same_cluster & earlier, scores, jnp.float32(-1.0)), axis=1)
        if want_columns:
            later = same_cluster & jnp.logical_not(earlier)
            col_best = jnp.max(jnp.where(later, scores, jnp.float32(-1.0)), axis=0)
        else:
            col_best = jnp.zeros((0,), jnp.float32)
        return (jnp.maximum(running, row_best), col_best)

    initial = jnp.full((row_emb.shape[0],), -1.0, jnp.float32)
    row_best, col_blocks = lax.scan(visit_block, initial, (emb_blocks, label_blocks, rank_blocks))
    return (row_best, col_blocks.reshape(-1))


def body(embeddings, labels, member_rank):
    row_count = embeddings.shape[0]
    feature_count = embeddings.shape[1]
    clus_count = lax.axis_size("clus")
    mem_count = lax.axis_size("mem")
    group_count = clus_count * mem_count
    capacity = 2 * row_count // group_count
    slot_count = group_count * capacity
    group_of = labels // CLUS_GROUP
    one_hot = (group_of[:, None] == jnp.arange(group_count, dtype=jnp.int32)[None, :]).astype(
        jnp.int32
    )
    running_count = jnp.cumsum(one_hot, axis=0) - 1
    within_group = jnp.sum(one_hot * running_count, axis=1)
    slot_of = group_of * capacity + within_group
    send_emb = jnp.zeros((slot_count, feature_count), jnp.bfloat16).at[slot_of].set(embeddings)
    send_label = jnp.full((slot_count,), -1, jnp.int32).at[slot_of].set(labels)
    send_rank = jnp.zeros((slot_count,), jnp.int32).at[slot_of].set(member_rank)
    received = (
        lax.all_to_all(
            send_emb.reshape(group_count, capacity, feature_count),
            ("clus", "mem"),
            split_axis=0,
            concat_axis=0,
            tiled=True,
        ),
        lax.all_to_all(
            send_label.reshape(group_count, capacity),
            ("clus", "mem"),
            split_axis=0,
            concat_axis=0,
            tiled=True,
        ),
        lax.all_to_all(
            send_rank.reshape(group_count, capacity),
            ("clus", "mem"),
            split_axis=0,
            concat_axis=0,
            tiled=True,
        ),
    )
    own_emb = received[0].reshape(slot_count, feature_count)
    own_label = received[1].reshape(slot_count)
    own_rank = received[2].reshape(slot_count)
    other_emb, other_label, other_rank = swapped((own_emb, own_label, own_rank), "sub", 0)
    diag_best, ignored = masked_best(
        own_emb, own_label, own_rank, own_emb, own_label, own_rank, False
    )
    core_side = lax.axis_index("sub")
    is_zero = core_side == 0
    zero_emb = jnp.where(is_zero, own_emb, other_emb)
    zero_label = jnp.where(is_zero, own_label, other_label)
    zero_rank = jnp.where(is_zero, own_rank, other_rank)
    one_emb = jnp.where(is_zero, other_emb, own_emb)
    one_label = jnp.where(is_zero, other_label, own_label)
    one_rank = jnp.where(is_zero, other_rank, own_rank)
    half_count = slot_count // 2
    offset = core_side * half_count
    part_emb = lax.dynamic_slice_in_dim(zero_emb, offset, half_count, 0)
    part_label = lax.dynamic_slice_in_dim(zero_label, offset, half_count, 0)
    part_rank = lax.dynamic_slice_in_dim(zero_rank, offset, half_count, 0)
    half_best, col_part = masked_best(
        part_emb, part_label, part_rank, one_emb, one_label, one_rank, True
    )
    got_half, got_cols = swapped((half_best, col_part), "sub", 0)
    row_side = jnp.concatenate([half_best, got_half])
    cross_best = jnp.where(is_zero, row_side, jnp.maximum(col_part, got_cols))
    nearest = jnp.maximum(diag_best, cross_best)
    returned = lax.all_to_all(
        nearest.reshape(group_count, capacity),
        ("clus", "mem"),
        split_axis=0,
        concat_axis=0,
        tiled=True,
    )
    return returned.reshape(-1)[slot_of]


def solution(mesh):
    placed = (
        P(("parts", "clus", "mem", "sub"), None),
        P(("parts", "clus", "mem", "sub")),
        P(("parts", "clus", "mem", "sub")),
    )
    return jax.shard_map(
        body,
        mesh=mesh,
        in_specs=placed,
        out_specs=P(("parts", "clus", "mem", "sub")),
        check_vma=False,
    )
```

profile of v0, /device:TPU:0, one launch (start us, length us, event | category | flops | bytes accessed | tf_op | source)
XLA Modules:
  0.0 60.0 jit_solution(17755115585680735418)
XLA Ops:
  0.0 0.7 %and_select_fusion = s32[128]{0:T(128)S(1)} fusion(s32[128]{0:T(128)} %param.4), kind=kLoop, calls=%fused_computation.25 | loop fusion | flops 1920 | bytes 1024 | tf_op jit(solution)/shard_map/jit(floor_divide)/jit(_where)/select_n | solution.py:53
  0.7 0.1 fusion.9
  0.8 0.2 reduce_window_sum.11
  0.9 0.0 copy-start
  0.9 0.2 select_reduce_fusion.2
  1.1 0.5 copy-done
  1.6 1.0 %scatter_custom_fusion = s32[256]{0:T(256)S(1)} fusion(s32[128]{0:T(128)S(1)} %compare_select_fusion, s32[128]{0:T(128)S(1)} %copy-done, s32[]{:T(128)} %constant.39.clone.1), kind=kCustom, calls=%fused_computation.39 | custom fusion | bytes 1028 | tf_op jit(solution)/shard_map/scatter | solution.py:61
  2.6 0.7 %all_to_all.21 = s32[8,1,32]{2,1,0:T(1,128)} reshape(s32[256]{0:T(256)S(1)} %scatter_custom_fusion) | data formatting | bytes 2048 | tf_op jit(solution)/shard_map/all_to_all | solution.py:71
  3.3 7.3 %all-to-all-start = ((s32[8,1,32]{2,1,0:T(1,128)}), s32[8,1,32]{2,1,0:T(1,128)S(1)}, u32[]{:S(2)}, u32[]{:S(2)}) async-start(s32[8,1,32]{2,1,0:T(1,128)} %all_to_all.21), calls=%async_computation | async-start | bytes 8192 | tf_op jit(solution)/shard_map/all_to_all | solution.py:71
  10.5 1.1 %scatter_custom_fusion.1 = s32[256]{0:T(256)S(1)} fusion(s32[128]{0:T(128)S(1)} %compare_select_fusion, s32[128]{0:T(128)} %param.5, s32[]{:T(128)} %constant.46.clone.1), kind=kCustom, calls=%fused_computation.35 | custom fusion | bytes 1536 | tf_op jit(solution)/shard_map/scatter | solution.py:62
  11.7 0.7 %all_to_all.23 = s32[8,1,32]{2,1,0:T(1,128)} reshape(s32[256]{0:T(256)S(1)} %scatter_custom_fusion.1) | data formatting | bytes 2048 | tf_op jit(solution)/shard_map/all_to_all | solution.py:78
  12.3 4.7 %all-to-all-done = s32[8,1,32]{2,1,0:T(1,128)S(1)} async-done(((s32[8,1,32]{2,1,0:T(1,128)}), s32[8,1,32]{2,1,0:T(1,128)S(1)}, u32[]{:S(2)}, u32[]{:S(2)}) %all-to-all-start) | async-done | bytes 1056 | tf_op jit(solution)/shard_map/all_to_all | solution.py:71
  17.0 3.3 %all-to-all-start.1 = ((s32[8,1,32]{2,1,0:T(1,128)}), s32[8,1,32]{2,1,0:T(1,128)S(1)}, u32[]{:S(2)}, u32[]{:S(2)}) async-start(s32[8,1,32]{2,1,0:T(1,128)} %all_to_all.23), calls=%async_computation.1 | async-start | bytes 8192 | tf_op jit(solution)/shard_map/all_to_all | solution.py:78
  20.4 2.4 %scatter_custom_fusion.2 = bf16[256,1024]{1,0:T(8,128)(2,1)} fusion(s32[128]{0:T(128)S(1)} %compare_select_fusion, bf16[128,1024]{1,0:T(8,128)(2,1)} %param.3, bf16[]{:T(256)} %constant.66.clone.1), kind=kCustom, calls=%fused_computation.11 | custom fusion | bytes 524800 | tf_op jit(solution)/shard_map/scatter | solution.py:60
  22.7 4.1 %all-to-all-done.1 = s32[8,1,32]{2,1,0:T(1,128)S(1)} async-done(((s32[8,1,32]{2,1,0:T(1,128)}), s32[8,1,32]{2,1,0:T(1,128)S(1)}, u32[]{:S(2)}, u32[]{:S(2)}) %all-to-all-start.1) | async-done | bytes 1056 | tf_op jit(solution)/shard_map/all_to_all | solution.py:78
  26.8 3.5 %all-to-all-start.2 = ((bf16[8,32,1024]{2,1,0:T(8,128)(2,1)}), bf16[8,32,1024]{2,1,0:T(8,128)(2,1)S(1)}, u32[]{:S(2)}, u32[]{:S(2)}) async-start(bf16[8,32,1024]{2,1,0:T(8,128)(2,1)} %bitcast), calls=%async_computation.2 | async-start | bytes 1048576 | tf_op jit(solution)/shard_map/all_to_all | solution.py:64
  30.3 0.5 broadcast.66
  30.8 0.7 %reduce.10 = s32[8,32]{1,0:T(8,128)S(1)} reduce(s32[8,1,32]{2,1,0:T(1,128)S(1)} %all-to-all-done, s32[]{:T(128)} %broadcast.66), dimensions={1}, to_apply=%all_to_all.22.reduce_sub_computation.3 | reduce | bytes 2052 | tf_op jit(solution)/shard_map/all_to_all | solution.py:71
  31.5 0.1 eq.61
  31.6 0.0 collective-permute-start
  31.6 0.7 %reduce.9 = s32[8,32]{1,0:T(8,128)S(1)} reduce(s32[8,1,32]{2,1,0:T(1,128)S(1)} %all-to-all-done.1, s32[]{:T(128)} %broadcast.66), dimensions={1}, to_apply=%all_to_all.24.reduce_sub_computation.3 | reduce | bytes 2052 | tf_op jit(solution)/shard_map/all_to_all | solution.py:78
  32.3 0.1 lt.56
  32.3 0.5 collective-permute-start.1
  32.8 9.6 %all-to-all-done.2 = bf16[8,32,1024]{2,1,0:T(8,128)(2,1)S(1)} async-done(((bf16[8,32,1024]{2,1,0:T(8,128)(2,1)}), bf16[8,32,1024]{2,1,0:T(8,128)(2,1)S(1)}, u32[]{:S(2)}, u32[]{:S(2)}) %all-to-all-start.2) | async-done | bytes 524320 | tf_op jit(solution)/shard_map/all_to_all | solution.py:64
  42.4 0.0 collective-permute-start.2
  42.4 0.0 collective-permute-done.1
  42.4 0.1 dynamic_slice.24
  42.5 0.0 collective-permute-done
  42.5 0.1 broadcast_compare_fusion.1
  42.6 1.7 %collective-permute-done.2 = bf16[256,1024]{1,0:T(8,128)(2,1)S(1)} collective-permute-done((bf16[256,1024]{1,0:T(8,128)(2,1)S(1)}, bf16[256,1024]{1,0:T(8,128)(2,1)S(1)}, u32[]{:S(2)}, u32[]{:S(2)}) %collective-permute-start.2) | collective-permute-done | bytes 524320 | tf_op jit(solution)/shard_map/ppermute | solution.py:14
  44.3 0.4 select_reduce_fusion
  44.7 0.2 collective-permute-start.3
  44.9 0.4 collective-permute-start.4
  45.3 0.4 fusion
  45.6 0.3 collective-permute-done.3
  45.9 0.2 collective-permute-done.4
  46.1 0.7 %all_to_all.26 = f32[8,1,32]{2,1,0:T(1,128)} reshape(f32[256]{0:T(256)S(1)} %fusion.10) | data formatting | bytes 2048 | tf_op jit(solution)/shard_map/all_to_all | solution.py:113
  46.8 3.7 %all-to-all-start.3 = ((f32[8,1,32]{2,1,0:T(1,128)}), f32[8,1,32]{2,1,0:T(1,128)S(1)}, u32[]{:S(2)}, u32[]{:S(2)}) async-start(f32[8,1,32]{2,1,0:T(1,128)} %all_to_all.26), calls=%async_computation.3 | async-start | bytes 8192 | tf_op jit(solution)/shard_map/all_to_all | solution.py:113
  50.5 6.5 %all-to-all-done.3 = f32[8,1,32]{2,1,0:T(1,128)S(1)} async-done(((f32[8,1,32]{2,1,0:T(1,128)}), f32[8,1,32]{2,1,0:T(1,128)S(1)}, u32[]{:S(2)}, u32[]{:S(2)}) %all-to-all-start.3) | async-done | bytes 1056 | tf_op jit(solution)/shard_map/all_to_all | solution.py:113
  57.0 0.5 broadcast.68
  57.5 0.7 %reduce.11 = f32[8,32]{1,0:T(8,128)S(1)} reduce(f32[8,1,32]{2,1,0:T(1,128)S(1)} %all-to-all-done.3, f32[]{:T(128)} %broadcast.68), dimensions={1}, to_apply=%all_to_all.27.reduce_sub_computation.3 | reduce | bytes 2052 | tf_op jit(solution)/shard_map/all_to_all | solution.py:113
  58.1 0.1 reshape.61
  58.2 1.8 %gather_fusion = f32[128]{0:T(128)} fusion(f32[256]{0:T(256)S(1)} %reshape.61, s32[1024]{0:T(1024)S(1)} %pad_clamp_fusion), kind=kCustom, calls=%fused_computation | custom fusion | bytes 1536 | tf_op jit(solution)/shard_map/gather | solution.py:120
  (7 shorter events, 0.0 us)
Async XLA Ops:
  0.9 0.7 %copy-start = (s32[128]{0:T(128)S(1)}, s32[128]{0:T(128)}, u32[]{:S(2)}) copy-start(s32[128]{0:T(128)} %param.4) | copy-start | bytes 1540
  3.3 13.8 %all-to-all-start = ((s32[8,1,32]{2,1,0:T(1,128)}), s32[8,1,32]{2,1,0:T(1,128)S(1)}, u32[]{:S(2)}, u32[]{:S(2)}) async-start(s32[8,1,32]{2,1,0:T(1,128)} %all_to_all.21), calls=%async_computation | async-start | bytes 8192 | tf_op jit(solution)/shard_map/all_to_all | solution.py:71
  17.0 9.8 %all-to-all-start.1 = ((s32[8,1,32]{2,1,0:T(1,128)}), s32[8,1,32]{2,1,0:T(1,128)S(1)}, u32[]{:S(2)}, u32[]{:S(2)}) async-start(s32[8,1,32]{2,1,0:T(1,128)} %all_to_all.23), calls=%async_computation.1 | async-start | bytes 8192 | tf_op jit(solution)/shard_map/all_to_all | solution.py:78
  26.8 15.6 %all-to-all-start.2 = ((bf16[8,32,1024]{2,1,0:T(8,128)(2,1)}), bf16[8,32,1024]{2,1,0:T(8,128)(2,1)S(1)}, u32[]{:S(2)}, u32[]{:S(2)}) async-start(bf16[8,32,1024]{2,1,0:T(8,128)(2,1)} %bitcast), calls=%async_computation.2 | async-start | bytes 1048576 | tf_op jit(solution)/shard_map/all_to_all | solution.py:64
  31.6 10.9 %collective-permute-start = (s32[256]{0:T(256)S(1)}, s32[256]{0:T(256)S(1)}, u32[]{:S(2)}, u32[]{:S(2)}) collective-permute-start(s32[256]{0:T(256)S(1)} %eq.61), channel_id=1, source_target_pairs={{0,1},{1,0},{2,3},{3,2},{4,5},{5,4},{6,7},{7,6},{8,9},{9,8},{10,11... | collective-permute-start | bytes 3080 | tf_op jit(solution)/shard_map/ppermute | solution.py:14
  32.3 10.1 %collective-permute-start.1 = (s32[256]{0:T(256)S(1)}, s32[256]{0:T(256)S(1)}, u32[]{:S(2)}, u32[]{:S(2)}) collective-permute-start(s32[256]{0:T(256)S(1)} %lt.56), channel_id=1, source_target_pairs={{0,1},{1,0},{2,3},{3,2},{4,5},{5,4},{6,7},{7,6},{8,9},{9,8},{10,11... | collective-permute-start | bytes 3080 | tf_op jit(solution)/shard_map/ppermute | solution.py:14
  42.4 1.9 %collective-permute-start.2 = (bf16[256,1024]{1,0:T(8,128)(2,1)S(1)}, bf16[256,1024]{1,0:T(8,128)(2,1)S(1)}, u32[]{:S(2)}, u32[]{:S(2)}) collective-permute-start(bf16[256,1024]{1,0:T(8,128)(2,1)S(1)} %bitcast.4), channel_id=1, source_target_pairs={{0,1},{1,0},{2,3},{3,2},{4,5},{5,4},{6,7},{7,6},{8,9},{9,8},{10,11... | collective-permute-start | bytes 1572872 | tf_op jit(solution)/shard_map/ppermute | solution.py:14
  44.7 1.2 %collective-permute-start.3 = (f32[128]{0:T(128)S(1)}, f32[128]{0:T(128)S(1)}, u32[]{:S(2)}, u32[]{:S(2)}) collective-permute-start(f32[128]{0:T(128)S(1)} %broadcast_maximum_fusion), channel_id=1, source_target_pairs={{0,1},{1,0},{2,3},{3,2},{4,5},{5,4},{6,7},{7,6},{8,9},{9,8},{10,11... | collective-permute-start | bytes 1544 | tf_op jit(solution)/shard_map/ppermute | solution.py:14
  44.9 1.2 %collective-permute-start.4 = (f32[256]{0:T(256)S(1)}, f32[256]{0:T(256)S(1)}, u32[]{:S(2)}, u32[]{:S(2)}) collective-permute-start(f32[256]{0:T(256)S(1)} %get-tuple-element.36), channel_id=1, source_target_pairs={{0,1},{1,0},{2,3},{3,2},{4,5},{5,4},{6,7},{7,6},{8,9},{9,8},{10,11... | collective-permute-start | bytes 3080 | tf_op jit(solution)/shard_map/ppermute | solution.py:14
  46.8 10.2 %all-to-all-start.3 = ((f32[8,1,32]{2,1,0:T(1,128)}), f32[8,1,32]{2,1,0:T(1,128)S(1)}, u32[]{:S(2)}, u32[]{:S(2)}) async-start(f32[8,1,32]{2,1,0:T(1,128)} %all_to_all.26), calls=%async_computation.3 | async-start | bytes 8192 | tf_op jit(solution)/shard_map/all_to_all | solution.py:113
where the time goes:
time: 60.4 us; the launch traced here: 60 us
  waiting for transfers between devices  27 us (45%)
  starting transfers between devices  18.9 us (31%)
  local copies, waits for them, and re-layouts  10.1 us (17%)
  other arithmetic  3.2 us (5%)
  matrix products  0.74 us (1%)
    all_to_all x1, waiting for transfers between devices, body(): lax.all_to_all(send_emb.reshape(group_count, capacity, feature_count), ('...  9.56 us
    all_to_all x1, starting transfers between devices, body(): lax.all_to_all(send_label.reshape(group_count, capacity), ('clus', 'mem')...  7.28 us
    all_to_all x1, waiting for transfers between devices, body(): lax.all_to_all(nearest.reshape(group_count, capacity), ('clus', 'mem'), s...  6.49 us
    all_to_all x1, waiting for transfers between devices, body(): lax.all_to_all(send_label.reshape(group_count, capacity), ('clus', 'mem')...  4.7 us
    all_to_all x1, waiting for transfers between devices, body(): lax.all_to_all(send_rank.reshape(group_count, capacity), ('clus', 'mem'),...  4.06 us
    all_to_all x1, starting transfers between devices, body(): lax.all_to_all(nearest.reshape(group_count, capacity), ('clus', 'mem'), s...  3.66 us
    all_to_all x1, starting transfers between devices, body(): lax.all_to_all(send_emb.reshape(group_count, capacity, feature_count), ('...  3.49 us
    all_to_all x1, starting transfers between devices, body(): lax.all_to_all(send_rank.reshape(group_count, capacity), ('clus', 'mem'),...  3.34 us
  transfers between devices with their start and end apart: 9, of which 7 were waited for; matrix products, arithmetic and copies ran while one was open for 10% of the time, Pallas kernels for 0%

commit v1 on v0

--- a/solution.py
+++ b/solution.py
@@ -1,11 +1,329 @@
+import functools
 import math
 
 import jax
 import jax.numpy as jnp
 from jax import lax
+from jax.experimental import pallas as pl
+from jax.experimental.pallas import tpu as pltpu
 from jax.sharding import PartitionSpec as P
 
 CLUS_GROUP = 2
+MESH = pl.DeviceIdType.MESH
+ROW_TILE = 16
+LANES = 128
+BYTE = 256
+CLASS_STEP = BYTE * BYTE
+
+
+def flipped(index, mask, size):
+    out = 0
+    bit = 1
+    while bit < size:
+        digit = lax.rem(lax.div(index, bit), 2)
+        out = out + ((1 - digit) if mask & bit else digit) * bit
+        bit *= 2
+    return out
+
+
+def nt_dot(lhs, rhs):
+    return lax.dot_general(lhs, rhs, (((1,), (1,)), ((), ())), preferred_element_type=jnp.float32)
+
+
+def dedup_kernel(
+    clus_count,
+    mem_count,
+    capacity,
+    emb_hbm,
+    label_ref,
+    rank_ref,
+    out_ref,
+    emb,
+    send,
+    own,
+    sib,
+    key_out,
+    key_in,
+    key_own,
+    key_sib,
+    ret_out,
+    ret_in,
+    load_sem,
+    emb_send,
+    emb_recv,
+    key_send,
+    key_recv,
+    fwd_send,
+    fwd_recv,
+    kf_send,
+    kf_recv,
+    ret_send,
+    ret_recv,
+):
+    groups = clus_count * mem_count
+    rows = emb.shape[0]
+    slots = groups * capacity
+    tiles = slots // LANES
+    per_tile = LANES // capacity
+    clus = lax.axis_index("clus")
+    mem = lax.axis_index("mem")
+    sub = lax.axis_index("sub")
+    me = clus * mem_count + mem
+
+    load = pltpu.make_async_copy(emb_hbm, emb, load_sem)
+    load.start()
+
+    def partner(k):
+        return {
+            "clus": flipped(clus, k // mem_count, clus_count),
+            "mem": flipped(mem, k % mem_count, mem_count),
+        }
+
+    sibling = {"sub": 1 - sub}
+    far_first = list(range(groups - 1, 0, -1))
+    barrier = pltpu.get_barrier_semaphore()
+    for k in far_first:
+        pl.semaphore_signal(barrier, inc=1, device_id=partner(k), device_id_type=MESH)
+    pl.semaphore_signal(barrier, inc=1, device_id=sibling, device_id_type=MESH)
+
+    labels = label_ref[...]
+    group = lax.div(labels, CLUS_GROUP)
+    relative = jnp.bitwise_xor(group, me)
+    group_iota = lax.broadcasted_iota(jnp.int32, (groups, rows), 0)
+    member = group_iota == relative
+    before = lax.broadcasted_iota(jnp.int32, (rows, rows), 0) < lax.broadcasted_iota(
+        jnp.int32, (rows, rows), 1
+    )
+    counts = jnp.dot(
+        member.astype(jnp.float32).astype(jnp.bfloat16),
+        before.astype(jnp.float32).astype(jnp.bfloat16),
+        preferred_element_type=jnp.float32,
+    )
+    slot = jnp.sum(
+        jnp.where(member, counts + (group_iota * capacity).astype(jnp.float32), 0.0),
+        axis=0,
+        keepdims=True,
+    ).astype(jnp.int32)
+    place = (
+        (lax.broadcasted_iota(jnp.int32, (slots, rows), 0) == slot)
+        .astype(jnp.float32)
+        .astype(jnp.bfloat16)
+    )
+
+    ranks = rank_ref[...]
+    row_iota = lax.broadcasted_iota(jnp.int32, (8, rows), 0)
+    digits = jnp.where(
+        row_iota == 0,
+        labels - group * CLUS_GROUP + 1,
+        jnp.where(
+            row_iota == 1,
+            lax.div(ranks, BYTE),
+            jnp.where(row_iota == 2, lax.rem(ranks, BYTE), 0),
+        ),
+    )
+    placed = nt_dot(digits.astype(jnp.float32).astype(jnp.bfloat16), place)
+    keys = placed[0:1] * float(CLASS_STEP) + placed[1:2] * float(BYTE) + placed[2:3]
+    for t in range(tiles):
+        key_out[t] = keys[:, t * LANES : (t + 1) * LANES]
+
+    load.wait()
+
+    def fill(first, count):
+        span = pl.ds(first * capacity, count * capacity)
+        send[span, :] = jnp.dot(
+            place[first * capacity : (first + count) * capacity],
+            emb[...],
+            preferred_element_type=jnp.float32,
+        ).astype(jnp.bfloat16)
+
+    def block(ref, k):
+        return ref.at[pl.ds(k * capacity, capacity), :]
+
+    emb_copies, key_copies = {}, {}
+    for k in far_first:
+        emb_copies[k] = pltpu.make_async_remote_copy(
+            src_ref=block(send, k),
+            dst_ref=block(own, k),
+            send_sem=emb_send.at[k],
+            recv_sem=emb_recv.at[k],
+            device_id=partner(k),
+            device_id_type=MESH,
+        )
+        key_copies[k] = pltpu.make_async_remote_copy(
+            src_ref=key_out.at[k // per_tile],
+            dst_ref=key_in.at[k],
+            send_sem=key_send.at[k],
+            recv_sem=key_recv.at[k],
+            device_id=partner(k),
+            device_id_type=MESH,
+        )
+    half = groups // 2
+    fill(half, half)
+    pl.semaphore_wait(barrier, groups)
+    for k in far_first:
+        key_copies[k].start()
+    for k in far_first[:half]:
+        emb_copies[k].start()
+    fill(0, half)
+    for k in far_first[half:]:
+        emb_copies[k].start()
+    own[pl.ds(0, capacity), :] = send[pl.ds(0, capacity), :]
+
+    forwards = {}
+    for k in range(groups):
+        forwards[k] = pltpu.make_async_remote_copy(
+            src_ref=block(send if k == 0 else own, k),
+            dst_ref=block(sib, k),
+            send_sem=fwd_send.at[k],
+            recv_sem=fwd_recv.at[k],
+            device_id=sibling,
+            device_id_type=MESH,
+        )
+    forwards[0].start()
+    lane_block = lax.div(lax.broadcasted_iota(jnp.int32, (1, LANES), 1), capacity)
+    for k in range(1, groups):
+        key_copies[k].wait_recv()
+    for t in range(tiles):
+        row = jnp.zeros((1, LANES), jnp.float32)
+        for k in range(t * per_tile, (t + 1) * per_tile):
+            piece = key_out[t] if k == 0 else key_in[k]
+            row = jnp.where(lane_block == k % per_tile, piece, row)
+        key_own[t] = row
+    key_forward = pltpu.make_async_remote_copy(
+        src_ref=key_own,
+        dst_ref=key_sib,
+        send_sem=kf_send,
+        recv_sem=kf_recv,
+        device_id=sibling,
+        device_id_type=MESH,
+    )
+    key_forward.start()
+    for k in range(1, groups):
+        emb_copies[k].wait_recv()
+        forwards[k].start()
+    key_forward.wait_recv()
+
+    row_keys = jnp.concatenate([key_own[t] for t in range(tiles)], axis=1)
+    row_base = (
+        lax.div(row_keys.astype(jnp.int32), CLASS_STEP) * CLASS_STEP
+    ).astype(jnp.float32)
+    row_base = jnp.maximum(row_base, 1.0)
+
+    def masked(cands, cand_keys):
+        scores = nt_dot(cands[...], own[...])
+        best = jnp.full((1, slots), -1.0, jnp.float32)
+        for t in range(tiles):
+            column = jnp.transpose(jnp.broadcast_to(cand_keys[t], (LANES, LANES)))
+            column = jnp.concatenate([column] * tiles, axis=1)
+            allowed = (column < row_keys) & (column >= row_base)
+            piece = jnp.where(allowed, scores[t * LANES : (t + 1) * LANES], -1.0)
+            best = jnp.maximum(best, jnp.max(piece, axis=0, keepdims=True))
+        return best
+
+    best = masked(own, key_own)
+    for k in range(groups):
+        forwards[k].wait_recv()
+    best = jnp.maximum(best, masked(sib, key_sib))
+    for t in range(tiles):
+        ret_out[t] = best[:, t * LANES : (t + 1) * LANES]
+
+    returns = {}
+    for k in far_first:
+        returns[k] = pltpu.make_async_remote_copy(
+            src_ref=ret_out.at[k // per_tile],
+            dst_ref=ret_in.at[k],
+            send_sem=ret_send.at[k],
+            recv_sem=ret_recv.at[k],
+            device_id=partner(k),
+            device_id_type=MESH,
+        )
+        returns[k].start()
+    for k in far_first:
+        emb_copies[k].wait_send()
+        key_copies[k].wait_send()
+    for k in range(groups):
+        forwards[k].wait_send()
+    key_forward.wait_send()
+    for k in range(1, groups):
+        returns[k].wait_recv()
+
+    pieces = []
+    for t in range(tiles):
+        row = jnp.zeros((1, LANES), jnp.float32)
+        for k in range(t * per_tile, (t + 1) * per_tile):
+            piece = ret_out[t] if k == 0 else ret_in[k]
+            row = jnp.where(lane_block == k % per_tile, piece, row)
+        pieces.append(row)
+    result = jnp.concatenate(pieces, axis=1)
+    high = result.astype(jnp.bfloat16).astype(jnp.float32)
+    middle = (result - high).astype(jnp.bfloat16).astype(jnp.float32)
+    low = result - high - middle
+    split_iota = lax.broadcasted_iota(jnp.int32, (8, slots), 0)
+    split = jnp.where(
+        split_iota == 0,
+        high,
+        jnp.where(split_iota == 1, middle, jnp.where(split_iota == 2, low, 0.0)),
+    ).astype(jnp.bfloat16)
+    taken = jnp.dot(split, place, preferred_element_type=jnp.float32)
+    out_ref[...] = taken[0:1] + taken[1:2] + taken[2:3]
+    for k in far_first:
+        returns[k].wait_send()
+
+
+def kernel_body(clus_count, mem_count, embeddings, labels, member_rank):
+    rows, width = embeddings.shape
+    groups = clus_count * mem_count
+    capacity = 2 * rows // groups
+    slots = groups * capacity
+    tiles = slots // LANES
+    dma = pltpu.SemaphoreType.DMA
+    vmem = pl.BlockSpec(memory_space=pltpu.VMEM)
+    out = pl.pallas_call(
+        functools.partial(dedup_kernel, clus_count, mem_count, capacity),
+        out_shape=jax.ShapeDtypeStruct((1, rows), jnp.float32),
+        in_specs=[pl.BlockSpec(memory_space=pl.ANY), vmem, vmem],
+        out_specs=vmem,
+        scratch_shapes=[
+            pltpu.VMEM((rows, width), jnp.bfloat16),
+            pltpu.VMEM((slots, width), jnp.bfloat16),
+            pltpu.VMEM((slots, width), jnp.bfloat16),
+            pltpu.VMEM((slots, width), jnp.bfloat16),
+            pltpu.VMEM((tiles, 1, LANES), jnp.float32),
+            pltpu.VMEM((groups, 1, LANES), jnp.float32),
+            pltpu.VMEM((tiles, 1, LANES), jnp.float32),
+            pltpu.VMEM((tiles, 1, LANES), jnp.float32),
+            pltpu.VMEM((tiles, 1, LANES), jnp.float32),
+            pltpu.VMEM((groups, 1, LANES), jnp.float32),
+            dma,
+            dma((groups,)),
+            dma((groups,)),
+            dma((groups,)),
+            dma((groups,)),
+            dma((groups,)),
+            dma((groups,)),
+            dma,
+            dma,
+            dma((groups,)),
+            dma((groups,)),
+        ],
+        compiler_params=pltpu.CompilerParams(collective_id=0, has_side_effects=True),
+    )(embeddings, labels.reshape(1, rows), member_rank.reshape(1, rows))
+    return out.reshape(rows)
+
+
+def fits_kernel(clus_count, mem_count, sub_count, rows):
+    groups = clus_count * mem_count
+    capacity = 2 * rows // groups
+    return (
+        clus_count & (clus_count - 1) == 0
+        and mem_count & (mem_count - 1) == 0
+        and sub_count == 2
+        and groups >= 2
+        and rows % LANES == 0
+        and capacity % ROW_TILE == 0
+        and LANES % capacity == 0
+        and rows * groups * sub_count <= CLASS_STEP
+    )
 
 
 def swapped(value, axis, stride):
@@ -120,6 +438,14 @@
     return returned.reshape(-1)[slot_of]
 
 
+def local(embeddings, labels, member_rank):
+    rows = embeddings.shape[0]
+    clus_count, mem_count, sub_count = (lax.axis_size(a) for a in ("clus", "mem", "sub"))
+    if fits_kernel(clus_count, mem_count, sub_count, rows):
+        return kernel_body(clus_count, mem_count, embeddings, labels, member_rank)
+    return body(embeddings, labels, member_rank)
+
+
 def solution(mesh):
     placed = (
         P(("parts", "clus", "mem", "sub"), None),
@@ -127,7 +453,7 @@
         P(("parts", "clus", "mem", "sub")),
     )
     return jax.shard_map(
-        body,
+        local,
         mesh=mesh,
         in_specs=placed,
         out_specs=P(("parts", "clus", "mem", "sub")),

time: 60.4 us -> 26.5 us (0.44)
  waiting for transfers between devices: 27 us -> 0 us
  Pallas kernels: 0 us -> 25.3 us
  starting transfers between devices: 18.9 us -> 0 us
  local copies, waits for them, and re-layouts: 10.1 us -> 1.1 us
  other arithmetic: 3.2 us -> 0 us
  matrix products: 0.74 us -> 0 us
    pallas_call x0 -> x1, Pallas kernels: none -> 25.3 us  [kernel_body(): pl.pallas_call(functools.partial(dedup_kernel, clus_count, mem_count, cap...]
    all_to_all x4 -> x0, waiting for transfers between devices: 24.8 us -> none  [the longest x1 9.56 us: body(): lax.all_to_all(send_emb.reshape(group_count, capacity, feature_count), ('...]
    all_to_all x4 -> x0, starting transfers between devices: 17.8 us -> none  [the longest x1 7.28 us: body(): lax.all_to_all(send_label.reshape(group_count, capacity), ('clus', 'mem')...]
    scatter x3 -> x0, local copies, waits for them, and re-layouts: 4.45 us -> none  [the longest x1 2.37 us: body(): jnp.zeros((slot_count, feature_count), jnp.bfloat16).at[slot_of]]
    all_to_all x5 -> x0, local copies, waits for them, and re-layouts: 3.05 us -> none  [the longest x2 1.19 us: body(): lax.all_to_all(nearest.reshape(group_count, capacity), ('clus', 'mem'), s...]
    ppermute x5 -> x0, waiting for transfers between devices: 2.2 us -> none  [swapped(): return lax.ppermute(value, axis, pairs)]
    all_to_all x3 -> x0, other arithmetic: 1.98 us -> none  [the longest x1 0.66 us: body(): lax.all_to_all(send_rank.reshape(group_count, capacity), ('clus', 'mem'),...]
    gather x1 -> x0, local copies, waits for them, and re-layouts: 1.76 us -> none  [body(): return returned.reshape(-1)[slot_of]]
  transfers between devices with their start and end apart: 9 -> 0, of which waited for: 7 -> 0; matrix products, arithmetic and copies ran while one was open for 10% -> 0% of each run, Pallas kernels for 0% -> 0%
where the time goes in v1:
time: 26.5 us; the launch traced here: 26.4 us
  Pallas kernels  25.3 us (95%)
  local copies, waits for them, and re-layouts  1.1 us (4%)
    pallas_call x1, Pallas kernels, kernel_body(): pl.pallas_call(functools.partial(dedup_kernel, clus_count, mem_count, cap...  25.3 us
    unnamed x3, local copies, waits for them, and re-layouts  1.1 us

profile of v1, /device:TPU:0, one launch (start us, length us, event | category | flops | bytes accessed | tf_op | source)
XLA Modules:
  0.0 26.4 jit_solution(17434962039788458223)
XLA Ops:
  0.0 25.3 %shard_map.37 = f32[1,128]{1,0:T(1,128)} custom-call(bf16[128,1024]{1,0:T(8,128)(2,1)} %emb_hbm.1, s32[1,128]{1,0:T(1,128)} %bitcast.3, s32[1,128]{1,0:T(1,128)} %bitcast.4), custom_call_target="tpu_custom_call" | custom-call | tf_op jit(solution)/shard_map/pallas_call | solution.py:281
  25.3 0.0 copy-start
  25.3 0.6 %copy-done = f32[1,128]{1,0:T(1,128)S(1)} copy-done((f32[1,128]{1,0:T(1,128)S(1)}, f32[1,128]{1,0:T(1,128)}, u32[]{:S(2)}) %copy-start) | copy-done | bytes 536
  25.9 0.5 %copy.5 = f32[128]{0:T(128)} copy(f32[128]{0:T(128)S(1)} %bitcast.5) | data formatting | bytes 1024
Async XLA Ops:
  25.3 0.6 %copy-start = (f32[1,128]{1,0:T(1,128)S(1)}, f32[1,128]{1,0:T(1,128)}, u32[]{:S(2)}) copy-start(f32[1,128]{1,0:T(1,128)} %shard_map.37) | copy-start | bytes 1540

commit v2 on v1

--- a/solution.py
+++ b/solution.py
@@ -14,6 +14,7 @@
 LANES = 128
 BYTE = 256
 CLASS_STEP = BYTE * BYTE
+NO_CAP = 3e38
 
 
 def flipped(index, mask, size):
@@ -35,10 +36,14 @@
     mem_count,
     capacity,
     emb_hbm,
+    label_hbm,
+    rank_hbm,
+    out_ref,
+    emb,
     label_ref,
     rank_ref,
-    out_ref,
-    emb,
+    caps_own,
+    caps_sib,
     send,
     own,
     sib,
@@ -70,8 +75,6 @@
     sub = lax.axis_index("sub")
     me = clus * mem_count + mem
 
-    load = pltpu.make_async_copy(emb_hbm, emb, load_sem)
-    load.start()
 
     def partner(k):
         return {
@@ -80,12 +83,19 @@
         }
 
     sibling = {"sub": 1 - sub}
+    load_label = pltpu.make_async_copy(label_hbm, label_ref, load_sem.at[0])
+    load_rank = pltpu.make_async_copy(rank_hbm, rank_ref, load_sem.at[1])
+    load = pltpu.make_async_copy(emb_hbm, emb, load_sem.at[2])
+    load_label.start()
+    load.start()
+    load_rank.start()
     far_first = list(range(groups - 1, 0, -1))
     barrier = pltpu.get_barrier_semaphore()
     for k in far_first:
         pl.semaphore_signal(barrier, inc=1, device_id=partner(k), device_id_type=MESH)
     pl.semaphore_signal(barrier, inc=1, device_id=sibling, device_id_type=MESH)
 
+    load_label.wait()
     labels = label_ref[...]
     group = lax.div(labels, CLUS_GROUP)
     relative = jnp.bitwise_xor(group, me)
@@ -109,22 +119,6 @@
         .astype(jnp.float32)
         .astype(jnp.bfloat16)
     )
-
-    ranks = rank_ref[...]
-    row_iota = lax.broadcasted_iota(jnp.int32, (8, rows), 0)
-    digits = jnp.where(
-        row_iota == 0,
-        labels - group * CLUS_GROUP + 1,
-        jnp.where(
-            row_iota == 1,
-            lax.div(ranks, BYTE),
-            jnp.where(row_iota == 2, lax.rem(ranks, BYTE), 0),
-        ),
-    )
-    placed = nt_dot(digits.astype(jnp.float32).astype(jnp.bfloat16), place)
-    keys = placed[0:1] * float(CLASS_STEP) + placed[1:2] * float(BYTE) + placed[2:3]
-    for t in range(tiles):
-        key_out[t] = keys[:, t * LANES : (t + 1) * LANES]
 
     load.wait()
 
@@ -160,10 +154,26 @@
     half = groups // 2
     fill(half, half)
     pl.semaphore_wait(barrier, groups)
-    for k in far_first:
-        key_copies[k].start()
     for k in far_first[:half]:
         emb_copies[k].start()
+    load_rank.wait()
+    ranks = rank_ref[...]
+    row_iota = lax.broadcasted_iota(jnp.int32, (8, rows), 0)
+    digits = jnp.where(
+        row_iota == 0,
+        labels - group * CLUS_GROUP + 1,
+        jnp.where(
+            row_iota == 1,
+            lax.div(ranks, BYTE),
+            jnp.where(row_iota == 2, lax.rem(ranks, BYTE), 0),
+        ),
+    )
+    placed = nt_dot(digits.astype(jnp.float32).astype(jnp.bfloat16), place)
+    keys = placed[0:1] * float(CLASS_STEP) + placed[1:2] * float(BYTE) + placed[2:3]
+    for t in range(tiles):
+        key_out[t] = keys[:, t * LANES : (t + 1) * LANES]
+    for k in far_first:
+        key_copies[k].start()
     fill(0, half)
     for k in far_first[half:]:
         emb_copies[k].start()
@@ -198,32 +208,36 @@
         device_id_type=MESH,
     )
     key_forward.start()
-    for k in range(1, groups):
-        emb_copies[k].wait_recv()
-        forwards[k].start()
-    key_forward.wait_recv()
-
     row_keys = jnp.concatenate([key_own[t] for t in range(tiles)], axis=1)
     row_base = (
         lax.div(row_keys.astype(jnp.int32), CLASS_STEP) * CLASS_STEP
     ).astype(jnp.float32)
     row_base = jnp.maximum(row_base, 1.0)
 
-    def masked(cands, cand_keys):
-        scores = nt_dot(cands[...], own[...])
-        best = jnp.full((1, slots), -1.0, jnp.float32)
+    def make_caps(caps, cand_keys):
         for t in range(tiles):
             column = jnp.transpose(jnp.broadcast_to(cand_keys[t], (LANES, LANES)))
             column = jnp.concatenate([column] * tiles, axis=1)
             allowed = (column < row_keys) & (column >= row_base)
-            piece = jnp.where(allowed, scores[t * LANES : (t + 1) * LANES], -1.0)
-            best = jnp.maximum(best, jnp.max(piece, axis=0, keepdims=True))
-        return best
-
-    best = masked(own, key_own)
-    for k in range(groups):
-        forwards[k].wait_recv()
-    best = jnp.maximum(best, masked(sib, key_sib))
+            caps[pl.ds(t * LANES, LANES), :] = jnp.where(allowed, NO_CAP, -1.0)
+
+    make_caps(caps_own, key_own)
+    key_forward.wait_recv()
+    make_caps(caps_sib, key_sib)
+
+    def masked(cands, caps, first, count):
+        span = pl.ds(first * capacity, count * capacity)
+        scores = jnp.minimum(nt_dot(cands[span, :], own[...]), caps[span, :])
+        return jnp.max(scores, axis=0, keepdims=True)
+
+    for k in range(1, groups):
+        emb_copies[k].wait_recv()
+        forwards[k].start()
+    best = jnp.maximum(masked(own, caps_own, 0, groups), -1.0)
+    for first in (0, half):
+        for k in range(first, first + half):
+            forwards[k].wait_recv()
+        best = jnp.maximum(best, masked(sib, caps_sib, first, half))
     for t in range(tiles):
         ret_out[t] = best[:, t * LANES : (t + 1) * LANES]
 
@@ -265,7 +279,7 @@
         jnp.where(split_iota == 1, middle, jnp.where(split_iota == 2, low, 0.0)),
     ).astype(jnp.bfloat16)
     taken = jnp.dot(split, place, preferred_element_type=jnp.float32)
-    out_ref[...] = taken[0:1] + taken[1:2] + taken[2:3]
+    out_ref[...] = taken
     for k in far_first:
         returns[k].wait_send()
 
@@ -280,11 +294,15 @@
     vmem = pl.BlockSpec(memory_space=pltpu.VMEM)
     out = pl.pallas_call(
         functools.partial(dedup_kernel, clus_count, mem_count, capacity),
-        out_shape=jax.ShapeDtypeStruct((1, rows), jnp.float32),
-        in_specs=[pl.BlockSpec(memory_space=pl.ANY), vmem, vmem],
+        out_shape=jax.ShapeDtypeStruct((8, rows), jnp.float32),
+        in_specs=[pl.BlockSpec(memory_space=pl.ANY)] * 3,
         out_specs=vmem,
         scratch_shapes=[
             pltpu.VMEM((rows, width), jnp.bfloat16),
+            pltpu.VMEM((1, rows), jnp.int32),
+            pltpu.VMEM((1, rows), jnp.int32),
+            pltpu.VMEM((slots, slots), jnp.float32),
+            pltpu.VMEM((slots, slots), jnp.float32),
             pltpu.VMEM((slots, width), jnp.bfloat16),
             pltpu.VMEM((slots, width), jnp.bfloat16),
             pltpu.VMEM((slots, width), jnp.bfloat16),
@@ -294,7 +312,7 @@
             pltpu.VMEM((tiles, 1, LANES), jnp.float32),
             pltpu.VMEM((tiles, 1, LANES), jnp.float32),
             pltpu.VMEM((groups, 1, LANES), jnp.float32),
-            dma,
+            dma((3,)),
             dma((groups,)),
             dma((groups,)),
             dma((groups,)),
@@ -308,7 +326,7 @@
         ],
         compiler_params=pltpu.CompilerParams(collective_id=0, has_side_effects=True),
     )(embeddings, labels.reshape(1, rows), member_rank.reshape(1, rows))
-    return out.reshape(rows)
+    return out[0] + out[1] + out[2]
 
 
 def fits_kernel(clus_count, mem_count, sub_count, rows):

time: 26.5 us -> 29 us (1.094)
  Pallas kernels: 25.3 us -> 27.5 us
  other arithmetic: 0 us -> 1.31 us
  local copies, waits for them, and re-layouts: 1.1 us -> 0 us
    pallas_call x1, Pallas kernels: 25.3 us -> 27.5 us  [kernel_body(): pl.pallas_call(functools.partial(dedup_kernel, clus_count, mem_count, cap...]
    add x0 -> x1, other arithmetic: none -> 1.31 us  [kernel_body(): return out[0] + out[1] + out[2]]
    unnamed x3 -> x0, local copies, waits for them, and re-layouts: 1.1 us -> none
where the time goes in v2:
time: 29 us; the launch traced here: 28.8 us
  Pallas kernels  27.5 us (95%)
  other arithmetic  1.31 us (5%)
    pallas_call x1, Pallas kernels, kernel_body(): pl.pallas_call(functools.partial(dedup_kernel, clus_count, mem_count, cap...  27.5 us
    add x1, other arithmetic, kernel_body(): return out[0] + out[1] + out[2]  1.31 us

profile of v2, /device:TPU:0, one launch (start us, length us, event | category | flops | bytes accessed | tf_op | source)
XLA Modules:
  0.0 28.8 jit_solution(4544465970541962977)
XLA Ops:
  0.0 27.5 %shard_map.37 = f32[8,128]{1,0:T(8,128)} custom-call(bf16[128,1024]{1,0:T(8,128)(2,1)} %emb_hbm.1, s32[1,128]{1,0:T(1,128)} %bitcast.4, s32[1,128]{1,0:T(1,128)} %bitcast.5), custom_call_target="tpu_custom_call" | custom-call | tf_op jit(solution)/shard_map/pallas_call | solution.py:295
  27.5 1.3 %add_bitcast_fusion = f32[128]{0:T(128)} fusion(f32[8,128]{1,0:T(8,128)} %shard_map.37), kind=kLoop, calls=%fused_computation | loop fusion | flops 256 | bytes 2048 | tf_op jit(solution)/shard_map/add | solution.py:329

commit v3 on v2

--- a/solution.py
+++ b/solution.py
@@ -120,8 +120,6 @@
         .astype(jnp.bfloat16)
     )
 
-    load.wait()
-
     def fill(first, count):
         span = pl.ds(first * capacity, count * capacity)
         send[span, :] = jnp.dot(
@@ -152,10 +150,6 @@
             device_id_type=MESH,
         )
     half = groups // 2
-    fill(half, half)
-    pl.semaphore_wait(barrier, groups)
-    for k in far_first[:half]:
-        emb_copies[k].start()
     load_rank.wait()
     ranks = rank_ref[...]
     row_iota = lax.broadcasted_iota(jnp.int32, (8, rows), 0)
@@ -172,8 +166,13 @@
     keys = placed[0:1] * float(CLASS_STEP) + placed[1:2] * float(BYTE) + placed[2:3]
     for t in range(tiles):
         key_out[t] = keys[:, t * LANES : (t + 1) * LANES]
+    load.wait()
+    fill(half, half)
+    pl.semaphore_wait(barrier, groups)
     for k in far_first:
         key_copies[k].start()
+    for k in far_first[:half]:
+        emb_copies[k].start()
     fill(0, half)
     for k in far_first[half:]:
         emb_copies[k].start()
@@ -279,7 +278,7 @@
         jnp.where(split_iota == 1, middle, jnp.where(split_iota == 2, low, 0.0)),
     ).astype(jnp.bfloat16)
     taken = jnp.dot(split, place, preferred_element_type=jnp.float32)
-    out_ref[...] = taken
+    out_ref[...] = taken[0:1] + taken[1:2] + taken[2:3]
     for k in far_first:
         returns[k].wait_send()
 
@@ -294,7 +293,7 @@
     vmem = pl.BlockSpec(memory_space=pltpu.VMEM)
     out = pl.pallas_call(
         functools.partial(dedup_kernel, clus_count, mem_count, capacity),
-        out_shape=jax.ShapeDtypeStruct((8, rows), jnp.float32),
+        out_shape=jax.ShapeDtypeStruct((1, rows), jnp.float32),
         in_specs=[pl.BlockSpec(memory_space=pl.ANY)] * 3,
         out_specs=vmem,
         scratch_shapes=[
@@ -326,7 +325,7 @@
         ],
         compiler_params=pltpu.CompilerParams(collective_id=0, has_side_effects=True),
     )(embeddings, labels.reshape(1, rows), member_rank.reshape(1, rows))
-    return out[0] + out[1] + out[2]
+    return out.reshape(rows)
 
 
 def fits_kernel(clus_count, mem_count, sub_count, rows):

time: 29 us -> 26.2 us (0.903)
  Pallas kernels: 27.5 us -> 24.9 us
  other arithmetic: 1.31 us -> 0 us
  local copies, waits for them, and re-layouts: 0 us -> 1.1 us
    pallas_call x1, Pallas kernels: 27.5 us -> 24.9 us  [kernel_body(): pl.pallas_call(functools.partial(dedup_kernel, clus_count, mem_count, cap...]
    add x1 -> x0, other arithmetic: 1.31 us -> none  [kernel_body(): return out[0] + out[1] + out[2]]
    unnamed x0 -> x3, local copies, waits for them, and re-layouts: none -> 1.1 us
where the time goes in v3:
time: 26.2 us; the launch traced here: 26 us
  Pallas kernels  24.9 us (95%)
  local copies, waits for them, and re-layouts  1.1 us (4%)
    pallas_call x1, Pallas kernels, kernel_body(): pl.pallas_call(functools.partial(dedup_kernel, clus_count, mem_count, cap...  24.9 us
    unnamed x3, local copies, waits for them, and re-layouts  1.1 us

profile of v3, /device:TPU:0, one launch (start us, length us, event | category | flops | bytes accessed | tf_op | source)
XLA Modules:
  0.0 26.0 jit_solution(9079485968971515131)
XLA Ops:
  0.0 24.9 %shard_map.37 = f32[1,128]{1,0:T(1,128)} custom-call(bf16[128,1024]{1,0:T(8,128)(2,1)} %emb_hbm.1, s32[1,128]{1,0:T(1,128)} %bitcast.3, s32[1,128]{1,0:T(1,128)} %bitcast.4), custom_call_target="tpu_custom_call" | custom-call | tf_op jit(solution)/shard_map/pallas_call | solution.py:294
  24.9 0.0 copy-start
  24.9 0.6 %copy-done = f32[1,128]{1,0:T(1,128)S(1)} copy-done((f32[1,128]{1,0:T(1,128)S(1)}, f32[1,128]{1,0:T(1,128)}, u32[]{:S(2)}) %copy-start) | copy-done | bytes 536
  25.5 0.5 %copy.5 = f32[128]{0:T(128)} copy(f32[128]{0:T(128)S(1)} %bitcast.5) | data formatting | bytes 1024
Async XLA Ops:
  24.9 0.6 %copy-start = (f32[1,128]{1,0:T(1,128)S(1)}, f32[1,128]{1,0:T(1,128)}, u32[]{:S(2)}) copy-start(f32[1,128]{1,0:T(1,128)} %shard_map.37) | copy-start | bytes 1540

commit v4 on v3

--- a/solution.py
+++ b/solution.py
@@ -128,6 +128,11 @@
             preferred_element_type=jnp.float32,
         ).astype(jnp.bfloat16)
 
+    def send_order(k):
+        clus_mask, mem_mask = divmod(k, mem_count)
+        near = clus_mask < clus_count // 2
+        return near, -clus_mask if near else clus_mask, -mem_mask
+
     def block(ref, k):
         return ref.at[pl.ds(k * capacity, capacity), :]
 
@@ -167,14 +172,11 @@
     for t in range(tiles):
         key_out[t] = keys[:, t * LANES : (t + 1) * LANES]
     load.wait()
-    fill(half, half)
+    fill(0, groups)
     pl.semaphore_wait(barrier, groups)
     for k in far_first:
         key_copies[k].start()
-    for k in far_first[:half]:
-        emb_copies[k].start()
-    fill(0, half)
-    for k in far_first[half:]:
+    for k in sorted(far_first, key=send_order):
         emb_copies[k].start()
     own[pl.ds(0, capacity), :] = send[pl.ds(0, capacity), :]
 

time: 26.2 us -> 25.3 us (0.966)
  Pallas kernels: 24.9 us -> 24.1 us
    pallas_call x1, Pallas kernels: 24.9 us -> 24.1 us  [kernel_body(): pl.pallas_call(functools.partial(dedup_kernel, clus_count, mem_count, cap...]
where the time goes in v4:
time: 25.3 us; the launch traced here: 25.2 us
  Pallas kernels  24.1 us (95%)
  local copies, waits for them, and re-layouts  1.1 us (4%)
    pallas_call x1, Pallas kernels, kernel_body(): pl.pallas_call(functools.partial(dedup_kernel, clus_count, mem_count, cap...  24.1 us
    unnamed x3, local copies, waits for them, and re-layouts  1.1 us

profile of v4, /device:TPU:0, one launch (start us, length us, event | category | flops | bytes accessed | tf_op | source)
XLA Modules:
  0.0 25.2 jit_solution(10638466157630005473)
XLA Ops:
  0.0 24.1 %shard_map.37 = f32[1,128]{1,0:T(1,128)} custom-call(bf16[128,1024]{1,0:T(8,128)(2,1)} %emb_hbm.1, s32[1,128]{1,0:T(1,128)} %bitcast.3, s32[1,128]{1,0:T(1,128)} %bitcast.4), custom_call_target="tpu_custom_call" | custom-call | tf_op jit(solution)/shard_map/pallas_call | solution.py:296
  24.1 0.0 copy-start
  24.1 0.6 %copy-done = f32[1,128]{1,0:T(1,128)S(1)} copy-done((f32[1,128]{1,0:T(1,128)S(1)}, f32[1,128]{1,0:T(1,128)}, u32[]{:S(2)}) %copy-start) | copy-done | bytes 536
  24.7 0.5 %copy.5 = f32[128]{0:T(128)} copy(f32[128]{0:T(128)S(1)} %bitcast.5) | data formatting | bytes 1024
Async XLA Ops:
  24.1 0.6 %copy-start = (f32[1,128]{1,0:T(1,128)S(1)}, f32[1,128]{1,0:T(1,128)}, u32[]{:S(2)}) copy-start(f32[1,128]{1,0:T(1,128)} %shard_map.37) | copy-start | bytes 1540

commit v5 on v4

--- a/solution.py
+++ b/solution.py
@@ -235,10 +235,9 @@
         emb_copies[k].wait_recv()
         forwards[k].start()
     best = jnp.maximum(masked(own, caps_own, 0, groups), -1.0)
-    for first in (0, half):
-        for k in range(first, first + half):
-            forwards[k].wait_recv()
-        best = jnp.maximum(best, masked(sib, caps_sib, first, half))
+    for k in range(groups):
+        forwards[k].wait_recv()
+    best = jnp.maximum(best, masked(sib, caps_sib, 0, groups))
     for t in range(tiles):
         ret_out[t] = best[:, t * LANES : (t + 1) * LANES]
 

time: 25.3 us -> 25 us (0.988)
  Pallas kernels: 24.1 us -> 23.7 us
    pallas_call x1, Pallas kernels: 24.1 us -> 23.7 us  [kernel_body(): pl.pallas_call(functools.partial(dedup_kernel, clus_count, mem_count, cap...]
where the time goes in v5:
time: 25 us; the launch traced here: 24.8 us
  Pallas kernels  23.7 us (95%)
  local copies, waits for them, and re-layouts  1.1 us (4%)
    pallas_call x1, Pallas kernels, kernel_body(): pl.pallas_call(functools.partial(dedup_kernel, clus_count, mem_count, cap...  23.7 us
    unnamed x3, local copies, waits for them, and re-layouts  1.1 us

profile of v5, /device:TPU:0, one launch (start us, length us, event | category | flops | bytes accessed | tf_op | source)
XLA Modules:
  0.0 24.8 jit_solution(13506614808256121595)
XLA Ops:
  0.0 23.7 %shard_map.37 = f32[1,128]{1,0:T(1,128)} custom-call(bf16[128,1024]{1,0:T(8,128)(2,1)} %emb_hbm.1, s32[1,128]{1,0:T(1,128)} %bitcast.3, s32[1,128]{1,0:T(1,128)} %bitcast.4), custom_call_target="tpu_custom_call" | custom-call | tf_op jit(solution)/shard_map/pallas_call | solution.py:295
  23.7 0.0 copy-start
  23.7 0.6 %copy-done = f32[1,128]{1,0:T(1,128)S(1)} copy-done((f32[1,128]{1,0:T(1,128)S(1)}, f32[1,128]{1,0:T(1,128)}, u32[]{:S(2)}) %copy-start) | copy-done | bytes 536
  24.3 0.5 %copy.5 = f32[128]{0:T(128)} copy(f32[128]{0:T(128)S(1)} %bitcast.5) | data formatting | bytes 1024
Async XLA Ops:
  23.7 0.6 %copy-start = (f32[1,128]{1,0:T(1,128)S(1)}, f32[1,128]{1,0:T(1,128)}, u32[]{:S(2)}) copy-start(f32[1,128]{1,0:T(1,128)} %shard_map.37) | copy-start | bytes 1540
